TPU v7x, 256 devices: a whole 4x4x8 slice. The times are simulated.
256 devices in a mesh: ctx: 64 (over x, z, core), head: 4 (over y).
Axes of the slice: x: 4, y: 4, z: 8, core: 2. Of those that a mesh axis runs over, the one named last changes fastest.
Arguments:
- mixer_input: bfloat16 [32768, 4096], P('ctx', 'head'), may hold values from -61 to 61
- gate_input: bfloat16 [32768, 4096], P('ctx', 'head'), may hold values from -7.5 to 7.5
- write_vecs: bfloat16 [32768, 128], P('ctx'), may hold values from -0.8984375 to 0.8984375
- read_vecs: bfloat16 [32768, 128], P('ctx'), may hold values from -0.8984375 to 0.8984375
- log_decay: float32 [64, 32768], P('head', 'ctx'), may hold values from -0.76 to 0
- doc_start: int32 [32768], P('ctx'), may hold values from 0 to 1, as said below
- live_mask: int32 [32768], P('ctx'), may hold values from 0 to 1, as said below
- skip_gain: float32 [64], P('head'), may hold values from 0.5 to 2
- norm_gain: float32 [4096], P('head'), may hold values from 0.25 to 1.75
- residual: bfloat16 [32768, 2048], P('ctx', 'head'), may hold values from -61 to 61
- out_weight: bfloat16 [4096, 2048], P(('head', 'ctx')), may hold values from -0.09375 to 0.09375
- mlp_gain: float32 [2048], replicated, may hold values from 0.25 to 1.75
- gate_weight: bfloat16 [2048, 4096], P('ctx', 'head'), may hold values from -0.125 to 0.125
- up_weight: bfloat16 [2048, 4096], P('ctx', 'head'), may hold values from -0.125 to 0.125
- down_weight: bfloat16 [4096, 2048], P(('head', 'ctx')), may hold values from -0.09375 to 0.09375
Outputs:
- mixed: bfloat16 [32768, 2048], P('ctx', 'head')
Inputs may be any that keep to these rules, and one draw needn't show every extreme that they name: `doc_start`: documents begin only at the first token of a group of 256; the window's first token begins one; a document spans at most 16 groups, and some document spans exactly that many. `live_mask`: the 0 entries are the tokens after a document's last real token, all within its last group; every document has a real token.
All inputs are finite; a program needn't handle non-finite values.
Results may differ from a plain program's by a relative error of at most 0.007.
Values may be sent and summed in bfloat16 or wider, within the bound.
No kernel may reach another device: no remote copies, remote signals or barrier semaphores. Data moves between devices by JAX's collectives and lax.ppermute only.
A program may use at most 128 MiB of HBM per device.

v0:
```python
import jax
import jax.numpy as jnp
from jax import lax
from jax.sharding import PartitionSpec as P

HDIM = 64
STATE = 128
GROUP = 256
DOC_GROUPS = 16
INNER = 4096
EPS = 1e-05


def passed_along(array, axis, by):
    peers = lax.axis_size(axis)
    pairs = [(i, i + by) for i in range(peers) if 0 <= i + by < peers]
    return lax.ppermute(array, axis, pairs)


def sent_together(arrays, axis, dim, along):
    widths = [a.shape[along] for a in arrays]
    both = jnp.concatenate(arrays, axis=along)
    filled = lax.all_gather(both, axis, axis=dim, tiled=True)
    return tuple(jnp.split(filled, [sum(widths[:k]) for k in range(1, len(widths))], axis=along))


def group_core(masked, write_group, read_group, log_group, start_group, skip_gain):
    positions = jnp.arange(GROUP)
    log_sums = jnp.cumsum(log_group, axis=1)
    doc_index = jnp.cumsum(start_group)
    same_doc = (doc_index[:, None] == doc_index[None, :]) & (
        positions[:, None] >= positions[None, :]
    )
    scores = jnp.dot(read_group, write_group.T, preferred_element_type=jnp.float32)
    log_gaps = jnp.where(same_doc[None], log_sums[:, :, None] - log_sums[:, None, :], 0.0)
    weights = jnp.where(same_doc[None], scores[None] * jnp.exp(log_gaps), 0.0).astype(jnp.bfloat16)
    per_head = masked.reshape(GROUP, -1, HDIM)
    intra_out = jnp.einsum("hij,jhp->ihp", weights, per_head, preferred_element_type=jnp.float32)
    tail_wts = (
        jnp.exp(log_sums[:, -1:] - log_sums)
        * (doc_index == doc_index[-1]).astype(jnp.float32)[None]
    )
    weighted = (write_group.astype(jnp.float32)[None] * tail_wts[:, :, None]).astype(jnp.bfloat16)
    local_state = jnp.einsum("hjn,jhp->hnp", weighted, per_head, preferred_element_type=jnp.float32)
    reach_wts = jnp.exp(log_sums) * (doc_index == 0).astype(jnp.float32)[None]
    decay_all = jnp.exp(log_sums[:, -1]) * (doc_index[-1] == 0).astype(jnp.float32)
    direct = intra_out + skip_gain[None, :, None] * per_head.astype(jnp.float32)
    return (direct, local_state, reach_wts, decay_all)


def shards(
    mixer_input,
    gate_input,
    write_vecs,
    read_vecs,
    log_decay,
    doc_start,
    live_mask,
    skip_gain,
    norm_gain,
    residual,
    out_weight,
    mlp_gain,
    gate_weight,
    up_weight,
    down_weight,
):
    tok_rows = mixer_input.shape[0]
    group_total = tok_rows // GROUP
    head_count = log_decay.shape[0]
    masked = mixer_input * live_mask.astype(jnp.bfloat16)[:, None]
    read_groups = read_vecs.reshape(group_total, GROUP, -1)
    group_data = (
        masked.reshape(group_total, GROUP, -1),
        write_vecs.reshape(group_total, GROUP, -1),
        read_groups,
        log_decay.reshape(head_count, group_total, GROUP).transpose(1, 0, 2),
        doc_start.reshape(group_total, GROUP),
    )

    def group_step(pieces):
        return group_core(pieces[0], pieces[1], pieces[2], pieces[3], pieces[4], skip_gain)

    directs, local_parts, reaches, decays = lax.map(group_step, group_data)
    run_state = jnp.zeros((head_count, STATE, HDIM), jnp.float32)
    run_factor = jnp.ones((head_count,), jnp.float32)
    before = []
    factors = []
    for group_id in range(group_total):
        before.append(run_state)
        factors.append(run_factor)
        run_state = decays[group_id][:, None, None] * run_state + local_parts[group_id]
        run_factor = run_factor * decays[group_id]
    hop_count = min(DOC_GROUPS // group_total + 1, lax.axis_size("ctx") - 1)

    def hop(hop_id, arriving):
        return passed_along(run_factor[:, None, None] * arriving + run_state, "ctx", 1)

    incoming = lax.fori_loop(0, hop_count, hop, jnp.zeros((head_count, STATE, HDIM), jnp.float32))
    outputs = []
    for group_id in range(group_total):
        inner_state = (factors[group_id][:, None, None] * incoming + before[group_id]).astype(
            jnp.bfloat16
        )
        crossed = jnp.einsum(
            "in,hnp->ihp", read_groups[group_id], inner_state, preferred_element_type=jnp.float32
        )
        outputs.append(directs[group_id] + crossed * reaches[group_id].T[:, :, None])
    output = jnp.concatenate(outputs, axis=0).reshape(tok_rows, -1)
    gated = output * jax.nn.silu(gate_input.astype(jnp.float32))
    squares = lax.psum(jnp.sum(gated * gated, axis=1), "head")
    normed = (gated * lax.rsqrt(squares / INNER + EPS)[:, None] * norm_gain).astype(jnp.bfloat16)
    width = out_weight.shape[1]
    columns = normed
    projected = jnp.dot(
        columns,
        lax.all_gather(out_weight, "ctx", axis=0, tiled=True),
        preferred_element_type=jnp.float32,
    )
    slice_width = residual.shape[1]
    offset = lax.axis_index("head") * slice_width
    placed = lax.dynamic_update_slice_in_dim(
        jnp.zeros((tok_rows, width), jnp.float32), residual.astype(jnp.float32), offset, 1
    )
    hidden_full = lax.psum(projected + placed, "head").astype(jnp.bfloat16)
    hidden_wide = hidden_full.astype(jnp.float32)
    row_scale = lax.rsqrt(jnp.mean(hidden_wide * hidden_wide, axis=1) + EPS)
    scaled = (hidden_wide * row_scale[:, None] * mlp_gain).astype(jnp.bfloat16)
    hidden = lax.dynamic_slice_in_dim(hidden_full, offset, slice_width, 1)
    pieces = sent_together((gate_weight, up_weight), "ctx", 0, 1)
    columns = scaled
    gate_out = jnp.dot(columns, pieces[0], preferred_element_type=jnp.float32)
    up_out = jnp.dot(columns, pieces[1], preferred_element_type=jnp.float32)
    act = (jax.nn.silu(gate_out) * up_out).astype(jnp.bfloat16)
    columns = act
    down_out = jnp.dot(
        columns,
        lax.all_gather(down_weight, "ctx", axis=0, tiled=True),
        preferred_element_type=jnp.float32,
    )
    mlp_part = lax.psum_scatter(
        down_out.astype(jnp.bfloat16), "head", scatter_dimension=1, tiled=True
    ).astype(jnp.float32)
    return (
        live_mask.astype(jnp.float32)[:, None] * (hidden.astype(jnp.float32) + mlp_part)
    ).astype(jnp.bfloat16)


def solution(mesh):
    return jax.shard_map(
        shards,
        mesh=mesh,
        in_specs=(
            P("ctx", "head"),
            P("ctx", "head"),
            P("ctx", None),
            P("ctx", None),
            P("head", "ctx"),
            P("ctx"),
            P("ctx"),
            P("head"),
            P("head"),
            P("ctx", "head"),
            P(("head", "ctx"), None),
            P(),
            P("ctx", "head"),
            P("ctx", "head"),
            P(("head", "ctx"), None),
        ),
        out_specs=P("ctx", "head"),
        check_vma=False,
    )
```

profile of v0, /device:TPU:1, one launch (start us, length us, event | category | flops | bytes accessed | tf_op | source)
XLA Modules:
  0.0 326.1 jit_solution(116184803706498684)
XLA Ops:
  15.1 27.7 %while.26 = (s32[]{:T(128)}, f32[2,256,16,64]{1,3,2,0:T(8,128)}, f32[2,16,128,64]{2,3,1,0:T(8,128)S(1)}, f32[2,16,256]{2,1,0:T(8,128)}, f32[2,16]{1,0:T(2,128)},...) while((s32[]{:T(128)}, f32[2,256,16,64]{1,3,2,0:T(8,128)}, ...), condition=%wide.region_5.6_spmd, body=%wide.region_0.5_spmd.sunk | while | flops 225981504 | bytes 7140167 | solution.py:84
  21.9 3.2 fusion.76
  35.7 3.2 fusion.76
  45.2 110.8 %while.27 = (s32[]{:T(128)}, f32[16,128,64]{1,2,0:T(8,128)S(1)}, f32[16]{0:T(128)S(1)}, f32[16,128,64]{1,2,0:T(8,128)S(1)}, s32[]{:T(128)}) while((s32[]{:T(128)}, f32[16,128,64]{1,2,0:T(8,128)S(1)}, f32[16]{0:T(128)S(1)}, f32[16,128,64]{1,2,0:T(8,128)S(1)}, s32[]{:T(128)}) %tuple.50), condition=%wide.region_7.8_spmd, body=%wide.region_6.7_spmd.sunk | while | flops 262146 | bytes 3670181 | solution.py:99
  45.4 4.9 %collective-permute-start = (f32[16,128,64]{1,2,0:T(8,128)S(1)}, f32[16,128,64]{1,2,0:T(8,128)S(1)}, u32[]{:S(2)}, u32[]{:S(2)}) collective-permute-start(f32[16,128,64]{1,2,0:T(8,128)S(1)} %multiply_add_fusion.2), channel_id=1, source_target_pairs={{0,4},{4,8},{8,12},{12,16},{16,20},{20,24},{24,28},{28,32},{32,36}... | collective-permute-start | bytes 1572872 | tf_op jit(solution)/shard_map/while/body/eval_jaxpr/ppermute | solution.py:17
  50.3 6.2 %collective-permute-done = f32[16,128,64]{1,2,0:T(8,128)S(1)} collective-permute-done((f32[16,128,64]{1,2,0:T(8,128)S(1)}, f32[16,128,64]{1,2,0:T(8,128)S(1)}, u32[]{:S(2)}, u32[]{:S(2)}) %collective-permute-start) | collective-permute-done | bytes 524320 | tf_op jit(solution)/shard_map/while/body/eval_jaxpr/ppermute | solution.py:17
  56.7 4.4 %collective-permute-start = (f32[16,128,64]{1,2,0:T(8,128)S(1)}, f32[16,128,64]{1,2,0:T(8,128)S(1)}, u32[]{:S(2)}, u32[]{:S(2)}) collective-permute-start(f32[16,128,64]{1,2,0:T(8,128)S(1)} %multiply_add_fusion.2), channel_id=1, source_target_pairs={{0,4},{4,8},{8,12},{12,16},{16,20},{20,24},{24,28},{28,32},{32,36}... | collective-permute-start | bytes 1572872 | tf_op jit(solution)/shard_map/while/body/eval_jaxpr/ppermute | solution.py:17
  61.1 8.1 %collective-permute-done = f32[16,128,64]{1,2,0:T(8,128)S(1)} collective-permute-done((f32[16,128,64]{1,2,0:T(8,128)S(1)}, f32[16,128,64]{1,2,0:T(8,128)S(1)}, u32[]{:S(2)}, u32[]{:S(2)}) %collective-permute-start) | collective-permute-done | bytes 524320 | tf_op jit(solution)/shard_map/while/body/eval_jaxpr/ppermute | solution.py:17
  69.3 4.5 %collective-permute-start = (f32[16,128,64]{1,2,0:T(8,128)S(1)}, f32[16,128,64]{1,2,0:T(8,128)S(1)}, u32[]{:S(2)}, u32[]{:S(2)}) collective-permute-start(f32[16,128,64]{1,2,0:T(8,128)S(1)} %multiply_add_fusion.2), channel_id=1, source_target_pairs={{0,4},{4,8},{8,12},{12,16},{16,20},{20,24},{24,28},{28,32},{32,36}... | collective-permute-start | bytes 1572872 | tf_op jit(solution)/shard_map/while/body/eval_jaxpr/ppermute | solution.py:17
  73.8 10.7 %collective-permute-done = f32[16,128,64]{1,2,0:T(8,128)S(1)} collective-permute-done((f32[16,128,64]{1,2,0:T(8,128)S(1)}, f32[16,128,64]{1,2,0:T(8,128)S(1)}, u32[]{:S(2)}, u32[]{:S(2)}) %collective-permute-start) | collective-permute-done | bytes 524320 | tf_op jit(solution)/shard_map/while/body/eval_jaxpr/ppermute | solution.py:17
  84.6 4.4 %collective-permute-start = (f32[16,128,64]{1,2,0:T(8,128)S(1)}, f32[16,128,64]{1,2,0:T(8,128)S(1)}, u32[]{:S(2)}, u32[]{:S(2)}) collective-permute-start(f32[16,128,64]{1,2,0:T(8,128)S(1)} %multiply_add_fusion.2), channel_id=1, source_target_pairs={{0,4},{4,8},{8,12},{12,16},{16,20},{20,24},{24,28},{28,32},{32,36}... | collective-permute-start | bytes 1572872 | tf_op jit(solution)/shard_map/while/body/eval_jaxpr/ppermute | solution.py:17
  89.0 6.4 %collective-permute-done = f32[16,128,64]{1,2,0:T(8,128)S(1)} collective-permute-done((f32[16,128,64]{1,2,0:T(8,128)S(1)}, f32[16,128,64]{1,2,0:T(8,128)S(1)}, u32[]{:S(2)}, u32[]{:S(2)}) %collective-permute-start) | collective-permute-done | bytes 524320 | tf_op jit(solution)/shard_map/while/body/eval_jaxpr/ppermute | solution.py:17
  95.4 4.4 %collective-permute-start = (f32[16,128,64]{1,2,0:T(8,128)S(1)}, f32[16,128,64]{1,2,0:T(8,128)S(1)}, u32[]{:S(2)}, u32[]{:S(2)}) collective-permute-start(f32[16,128,64]{1,2,0:T(8,128)S(1)} %multiply_add_fusion.2), channel_id=1, source_target_pairs={{0,4},{4,8},{8,12},{12,16},{16,20},{20,24},{24,28},{28,32},{32,36}... | collective-permute-start | bytes 1572872 | tf_op jit(solution)/shard_map/while/body/eval_jaxpr/ppermute | solution.py:17
  99.8 6.1 %collective-permute-done = f32[16,128,64]{1,2,0:T(8,128)S(1)} collective-permute-done((f32[16,128,64]{1,2,0:T(8,128)S(1)}, f32[16,128,64]{1,2,0:T(8,128)S(1)}, u32[]{:S(2)}, u32[]{:S(2)}) %collective-permute-start) | collective-permute-done | bytes 524320 | tf_op jit(solution)/shard_map/while/body/eval_jaxpr/ppermute | solution.py:17
  106.1 4.4 %collective-permute-start = (f32[16,128,64]{1,2,0:T(8,128)S(1)}, f32[16,128,64]{1,2,0:T(8,128)S(1)}, u32[]{:S(2)}, u32[]{:S(2)}) collective-permute-start(f32[16,128,64]{1,2,0:T(8,128)S(1)} %multiply_add_fusion.2), channel_id=1, source_target_pairs={{0,4},{4,8},{8,12},{12,16},{16,20},{20,24},{24,28},{28,32},{32,36}... | collective-permute-start | bytes 1572872 | tf_op jit(solution)/shard_map/while/body/eval_jaxpr/ppermute | solution.py:17
  110.5 7.8 %collective-permute-done = f32[16,128,64]{1,2,0:T(8,128)S(1)} collective-permute-done((f32[16,128,64]{1,2,0:T(8,128)S(1)}, f32[16,128,64]{1,2,0:T(8,128)S(1)}, u32[]{:S(2)}, u32[]{:S(2)}) %collective-permute-start) | collective-permute-done | bytes 524320 | tf_op jit(solution)/shard_map/while/body/eval_jaxpr/ppermute | solution.py:17
  118.3 4.4 %collective-permute-start = (f32[16,128,64]{1,2,0:T(8,128)S(1)}, f32[16,128,64]{1,2,0:T(8,128)S(1)}, u32[]{:S(2)}, u32[]{:S(2)}) collective-permute-start(f32[16,128,64]{1,2,0:T(8,128)S(1)} %multiply_add_fusion.2), channel_id=1, source_target_pairs={{0,4},{4,8},{8,12},{12,16},{16,20},{20,24},{24,28},{28,32},{32,36}... | collective-permute-start | bytes 1572872 | tf_op jit(solution)/shard_map/while/body/eval_jaxpr/ppermute | solution.py:17
  122.7 7.6 %collective-permute-done = f32[16,128,64]{1,2,0:T(8,128)S(1)} collective-permute-done((f32[16,128,64]{1,2,0:T(8,128)S(1)}, f32[16,128,64]{1,2,0:T(8,128)S(1)}, u32[]{:S(2)}, u32[]{:S(2)}) %collective-permute-start) | collective-permute-done | bytes 524320 | tf_op jit(solution)/shard_map/while/body/eval_jaxpr/ppermute | solution.py:17
  130.4 4.4 %collective-permute-start = (f32[16,128,64]{1,2,0:T(8,128)S(1)}, f32[16,128,64]{1,2,0:T(8,128)S(1)}, u32[]{:S(2)}, u32[]{:S(2)}) collective-permute-start(f32[16,128,64]{1,2,0:T(8,128)S(1)} %multiply_add_fusion.2), channel_id=1, source_target_pairs={{0,4},{4,8},{8,12},{12,16},{16,20},{20,24},{24,28},{28,32},{32,36}... | collective-permute-start | bytes 1572872 | tf_op jit(solution)/shard_map/while/body/eval_jaxpr/ppermute | solution.py:17
  134.8 6.1 %collective-permute-done = f32[16,128,64]{1,2,0:T(8,128)S(1)} collective-permute-done((f32[16,128,64]{1,2,0:T(8,128)S(1)}, f32[16,128,64]{1,2,0:T(8,128)S(1)}, u32[]{:S(2)}, u32[]{:S(2)}) %collective-permute-start) | collective-permute-done | bytes 524320 | tf_op jit(solution)/shard_map/while/body/eval_jaxpr/ppermute | solution.py:17
  141.1 4.4 %collective-permute-start = (f32[16,128,64]{1,2,0:T(8,128)S(1)}, f32[16,128,64]{1,2,0:T(8,128)S(1)}, u32[]{:S(2)}, u32[]{:S(2)}) collective-permute-start(f32[16,128,64]{1,2,0:T(8,128)S(1)} %multiply_add_fusion.2), channel_id=1, source_target_pairs={{0,4},{4,8},{8,12},{12,16},{16,20},{20,24},{24,28},{28,32},{32,36}... | collective-permute-start | bytes 1572872 | tf_op jit(solution)/shard_map/while/body/eval_jaxpr/ppermute | solution.py:17
  145.5 10.6 %collective-permute-done = f32[16,128,64]{1,2,0:T(8,128)S(1)} collective-permute-done((f32[16,128,64]{1,2,0:T(8,128)S(1)}, f32[16,128,64]{1,2,0:T(8,128)S(1)}, u32[]{:S(2)}, u32[]{:S(2)}) %collective-permute-start) | collective-permute-done | bytes 524320 | tf_op jit(solution)/shard_map/while/body/eval_jaxpr/ppermute | solution.py:17
  156.0 1.7 fusion.35
  160.8 2.0 copy.49
  163.6 9.8 %psum.14 = f32[512]{0:T(512)S(1)} all-reduce(f32[512]{0:T(512)S(1)} %multiply_reduce_fusion.1), channel_id=1, replica_groups=mesh['ctx'=64,'head'=4] {'head'}, use_global_device_ids=true, to_apply=%region_9.10 | all-reduce | flops 512 | bytes 4096 | tf_op jit(solution)/shard_map/psum | solution.py:111
  173.4 7.1 %fusion.40 = f32[512,2048]{1,0:T(8,128)} fusion(bf16[1024,2048]{1,0:T(8,128)(2,1)} %all-gather.4.cloned.1.call-done, f32[1024]{0:T(1024)S(1)} %copy-done.15, f32[512]{0:T(512)S(1)} %add_rsqrt_fusion.1, f32[512,1024]{1,0:T(8,128)S(1)} %copy.49, bf16[512,1024]{1,0:T(8,128)(2,1)S(1)} %copy-done.3), kind=kOutput, calls=%fused_computation.68 | convolution fusion | flops 2152202240 | bytes 11540480 | tf_op jit(solution)/shard_map/dot_general | solution.py:115
  180.5 2.5 add_dynamic-update-slice_fusion
  183.0 67.1 %all-reduce.1 = bf16[512,2048]{1,0:T(8,128)(2,1)S(1)} all-reduce(f32[512,2048]{1,0:T(8,128)} %add_dynamic-update-slice_fusion), channel_id=1, replica_groups=mesh['ctx'=64,'head'=4] {'head'}, use_global_device_ids=true, to_apply=%region_10.11 | all-reduce | flops 1048576 | bytes 6291456 | tf_op jit(solution)/shard_map/psum | solution.py:125
  250.8 5.9 %fusion.26 = f32[512,1024]{1,0:T(8,128)} fusion(bf16[2048,2048]{1,0:T(8,128)(2,1)} %all-gather.6.cloned.1.call-done, bf16[512,2048]{1,0:T(8,128)(2,1)S(1)} %all-reduce.1, f32[2048]{0:T(1024)S(1)} %copy-done.14, f32[512]{0:T(512)S(1)} %add_rsqrt_fusion), kind=kOutput, calls=%fused_computation.49 | convolution fusion | flops 2151677952 | bytes 8398848 | tf_op jit(solution)/shard_map/dot_general | solution.py:132
  258.0 10.0 %convolution_convert_fusion = bf16[512,2048]{1,0:T(8,128)(2,1)} fusion(bf16[1024,2048]{1,0:T(8,128)(2,1)} %all-gather.8.cloned.1.call-done, f32[512,1024]{1,0:T(8,128)} %fusion.26, bf16[2048,2048]{1,0:T(8,128)(2,1)} %all-gather.6.cloned.1.call-done, bf16[512,2048]{1,0:T(8,128)(2,1)S(1)} %all-reduce.1, f32[2048]{0:T(1024)S(1)} %copy-done.14, ...), kind=kOutput, calls=%fused_computation.51 | convolution fusion | flops 4303355904 | bytes 14690304 | tf_op jit(solution)/shard_map/dot_general | solution.py:136
  268.0 49.5 %reduce-scatter.2.cloned.1.call-done = bf16[512,512]{1,0:T(8,128)(2,1)} async-done(((bf16[512,2048]{1,0:T(8,128)(2,1)}), bf16[512,512]{1,0:T(8,128)(2,1)}) %reduce-scatter.2.cloned.1.call-update) | async-done | bytes 524304 | tf_op jit(solution)/shard_map/reduce_scatter | solution.py:141
  317.6 2.0 multiply_convert_fusion.5
  (146 shorter events, 37.3 us)
Async XLA Ops:
  6.5 8.5 %copy-start = (bf16[512,128]{1,0:T(8,128)(2,1)S(1)}, bf16[512,128]{1,0:T(8,128)(2,1)}, u32[]{:S(2)}) copy-start(bf16[512,128]{1,0:T(8,128)(2,1)} %param.21) | copy-start | bytes 393220
  6.5 166.8 %all-gather.4.cloned.1.call-start = ((), (), s32[]{:S(2)}) async-start(), calls=%async_computation.1 | async-start | bytes 4259840 | tf_op jit(solution)/shard_map/all_gather | solution.py:117
  7.3 243.3 %all-gather.6.cloned.1.call-start = ((), (), s32[]{:S(2)}) async-start(), calls=%async_computation.2 | async-start | bytes 8519680 | tf_op jit(solution)/shard_map/all_gather | solution.py:23
  8.9 249.2 %all-gather.8.cloned.1.call-start = ((), (), s32[]{:S(2)}) async-start(), calls=%async_computation.3 | async-start | bytes 4259840 | tf_op jit(solution)/shard_map/all_gather | solution.py:138
  9.6 308.0 %reduce-scatter.2.cloned.1.call-start = ((), (), s32[]{:S(2)}) async-start(), calls=%async_computation.4 | async-start | bytes 2621440 | tf_op jit(solution)/shard_map/reduce_scatter | solution.py:141
  21.8 3.2 copy-start.7
  21.8 4.5 %copy-start.4 = (f32[2,2,8,128]{3,2,0,1:T(8,128)S(1)}, f32[2,2,8,128]{3,2,0,1:T(8,128)}, u32[]{:S(2)}) copy-start(f32[2,2,8,128]{3,2,0,1:T(8,128)} %copy.65) | copy-start | bytes 49156 | tf_op jit(solution)/shard_map/while
  21.9 6.3 %copy-start.12 = (f32[2,16]{1,0:T(2,128)S(1)}, f32[2,16]{1,0:T(2,128)}, u32[]{:S(2)}) copy-start(f32[2,16]{1,0:T(2,128)} %get-tuple-element.291) | copy-start | bytes 388 | tf_op jit(solution)/shard_map/while
  21.9 6.4 %copy-start.2 = (f32[16,2,128]{2,0,1:T(8,128)S(1)}, f32[16,2,128]{2,0,1:T(8,128)}, u32[]{:S(2)}) copy-start(f32[16,2,128]{2,0,1:T(8,128)} %get-tuple-element.266) | copy-start | bytes 49156 | tf_op jit(solution)/shard_map/while
  21.9 6.4 %copy-start.8 = (f32[256]{0:T(256)S(1)}, f32[256]{0:T(256)}, u32[]{:S(2)}) copy-start(f32[256]{0:T(256)} %get-tuple-element.267) | copy-start | bytes 3076 | tf_op jit(solution)/shard_map/while
  21.9 6.4 %copy-start.9 = (f32[2,16,256]{2,1,0:T(8,128)S(1)}, f32[2,16,256]{2,1,0:T(8,128)}, u32[]{:S(2)}) copy-start(f32[2,16,256]{2,1,0:T(8,128)} %get-tuple-element.290) | copy-start | bytes 98308 | tf_op jit(solution)/shard_map/while
  33.7 1.8 copy-start.6
  35.7 3.2 copy-start.7
  35.7 4.6 %copy-start.4 = (f32[2,2,8,128]{3,2,0,1:T(8,128)S(1)}, f32[2,2,8,128]{3,2,0,1:T(8,128)}, u32[]{:S(2)}) copy-start(f32[2,2,8,128]{3,2,0,1:T(8,128)} %copy.65) | copy-start | bytes 49156 | tf_op jit(solution)/shard_map/while
  35.7 6.3 %copy-start.12 = (f32[2,16]{1,0:T(2,128)S(1)}, f32[2,16]{1,0:T(2,128)}, u32[]{:S(2)}) copy-start(f32[2,16]{1,0:T(2,128)} %get-tuple-element.291) | copy-start | bytes 388 | tf_op jit(solution)/shard_map/while
  35.7 6.4 %copy-start.2 = (f32[16,2,128]{2,0,1:T(8,128)S(1)}, f32[16,2,128]{2,0,1:T(8,128)}, u32[]{:S(2)}) copy-start(f32[16,2,128]{2,0,1:T(8,128)} %get-tuple-element.266) | copy-start | bytes 49156 | tf_op jit(solution)/shard_map/while
  35.7 6.4 %copy-start.8 = (f32[256]{0:T(256)S(1)}, f32[256]{0:T(256)}, u32[]{:S(2)}) copy-start(f32[256]{0:T(256)} %get-tuple-element.267) | copy-start | bytes 3076 | tf_op jit(solution)/shard_map/while
  35.7 6.4 %copy-start.9 = (f32[2,16,256]{2,1,0:T(8,128)S(1)}, f32[2,16,256]{2,1,0:T(8,128)}, u32[]{:S(2)}) copy-start(f32[2,16,256]{2,1,0:T(8,128)} %get-tuple-element.290) | copy-start | bytes 98308 | tf_op jit(solution)/shard_map/while
  45.4 11.2 %collective-permute-start = (f32[16,128,64]{1,2,0:T(8,128)S(1)}, f32[16,128,64]{1,2,0:T(8,128)S(1)}, u32[]{:S(2)}, u32[]{:S(2)}) collective-permute-start(f32[16,128,64]{1,2,0:T(8,128)S(1)} %multiply_add_fusion.2), channel_id=1, source_target_pairs={{0,4},{4,8},{8,12},{12,16},{16,20},{20,24},{24,28},{28,32},{32,36}... | collective-permute-start | bytes 1572872 | tf_op jit(solution)/shard_map/while/body/eval_jaxpr/ppermute | solution.py:17
  56.7 12.5 %collective-permute-start = (f32[16,128,64]{1,2,0:T(8,128)S(1)}, f32[16,128,64]{1,2,0:T(8,128)S(1)}, u32[]{:S(2)}, u32[]{:S(2)}) collective-permute-start(f32[16,128,64]{1,2,0:T(8,128)S(1)} %multiply_add_fusion.2), channel_id=1, source_target_pairs={{0,4},{4,8},{8,12},{12,16},{16,20},{20,24},{24,28},{28,32},{32,36}... | collective-permute-start | bytes 1572872 | tf_op jit(solution)/shard_map/while/body/eval_jaxpr/ppermute | solution.py:17
  69.3 15.2 %collective-permute-start = (f32[16,128,64]{1,2,0:T(8,128)S(1)}, f32[16,128,64]{1,2,0:T(8,128)S(1)}, u32[]{:S(2)}, u32[]{:S(2)}) collective-permute-start(f32[16,128,64]{1,2,0:T(8,128)S(1)} %multiply_add_fusion.2), channel_id=1, source_target_pairs={{0,4},{4,8},{8,12},{12,16},{16,20},{20,24},{24,28},{28,32},{32,36}... | collective-permute-start | bytes 1572872 | tf_op jit(solution)/shard_map/while/body/eval_jaxpr/ppermute | solution.py:17
  84.6 10.8 %collective-permute-start = (f32[16,128,64]{1,2,0:T(8,128)S(1)}, f32[16,128,64]{1,2,0:T(8,128)S(1)}, u32[]{:S(2)}, u32[]{:S(2)}) collective-permute-start(f32[16,128,64]{1,2,0:T(8,128)S(1)} %multiply_add_fusion.2), channel_id=1, source_target_pairs={{0,4},{4,8},{8,12},{12,16},{16,20},{20,24},{24,28},{28,32},{32,36}... | collective-permute-start | bytes 1572872 | tf_op jit(solution)/shard_map/while/body/eval_jaxpr/ppermute | solution.py:17
  95.4 10.5 %collective-permute-start = (f32[16,128,64]{1,2,0:T(8,128)S(1)}, f32[16,128,64]{1,2,0:T(8,128)S(1)}, u32[]{:S(2)}, u32[]{:S(2)}) collective-permute-start(f32[16,128,64]{1,2,0:T(8,128)S(1)} %multiply_add_fusion.2), channel_id=1, source_target_pairs={{0,4},{4,8},{8,12},{12,16},{16,20},{20,24},{24,28},{28,32},{32,36}... | collective-permute-start | bytes 1572872 | tf_op jit(solution)/shard_map/while/body/eval_jaxpr/ppermute | solution.py:17
  106.1 12.2 %collective-permute-start = (f32[16,128,64]{1,2,0:T(8,128)S(1)}, f32[16,128,64]{1,2,0:T(8,128)S(1)}, u32[]{:S(2)}, u32[]{:S(2)}) collective-permute-start(f32[16,128,64]{1,2,0:T(8,128)S(1)} %multiply_add_fusion.2), channel_id=1, source_target_pairs={{0,4},{4,8},{8,12},{12,16},{16,20},{20,24},{24,28},{28,32},{32,36}... | collective-permute-start | bytes 1572872 | tf_op jit(solution)/shard_map/while/body/eval_jaxpr/ppermute | solution.py:17
  118.3 12.0 %collective-permute-start = (f32[16,128,64]{1,2,0:T(8,128)S(1)}, f32[16,128,64]{1,2,0:T(8,128)S(1)}, u32[]{:S(2)}, u32[]{:S(2)}) collective-permute-start(f32[16,128,64]{1,2,0:T(8,128)S(1)} %multiply_add_fusion.2), channel_id=1, source_target_pairs={{0,4},{4,8},{8,12},{12,16},{16,20},{20,24},{24,28},{28,32},{32,36}... | collective-permute-start | bytes 1572872 | tf_op jit(solution)/shard_map/while/body/eval_jaxpr/ppermute | solution.py:17
  130.4 10.5 %collective-permute-start = (f32[16,128,64]{1,2,0:T(8,128)S(1)}, f32[16,128,64]{1,2,0:T(8,128)S(1)}, u32[]{:S(2)}, u32[]{:S(2)}) collective-permute-start(f32[16,128,64]{1,2,0:T(8,128)S(1)} %multiply_add_fusion.2), channel_id=1, source_target_pairs={{0,4},{4,8},{8,12},{12,16},{16,20},{20,24},{24,28},{28,32},{32,36}... | collective-permute-start | bytes 1572872 | tf_op jit(solution)/shard_map/while/body/eval_jaxpr/ppermute | solution.py:17
  141.1 15.0 %collective-permute-start = (f32[16,128,64]{1,2,0:T(8,128)S(1)}, f32[16,128,64]{1,2,0:T(8,128)S(1)}, u32[]{:S(2)}, u32[]{:S(2)}) collective-permute-start(f32[16,128,64]{1,2,0:T(8,128)S(1)} %multiply_add_fusion.2), channel_id=1, source_target_pairs={{0,4},{4,8},{8,12},{12,16},{16,20},{20,24},{24,28},{28,32},{32,36}... | collective-permute-start | bytes 1572872 | tf_op jit(solution)/shard_map/while/body/eval_jaxpr/ppermute | solution.py:17
  156.0 2.0 copy-start.1
  160.8 2.1 copy-start.3
  162.8 10.5 %copy-start.15 = (f32[1024]{0:T(1024)S(1)}, f32[1024]{0:T(1024)}, u32[]{:S(2)}) copy-start(f32[1024]{0:T(1024)} %param.27) | copy-start | bytes 12292
  173.4 7.1 %copy-start.5 = (bf16[512,512]{1,0:T(8,128)(2,1)S(1)}, bf16[512,512]{1,0:T(8,128)(2,1)}, u32[]{:S(2)}) copy-start(bf16[512,512]{1,0:T(8,128)(2,1)} %param.28) | copy-start | bytes 1572868
  268.0 49.6 %copy-start.11 = (f32[512]{0:T(512)S(1)}, f32[512]{0:T(512)}, u32[]{:S(2)}) copy-start(f32[512]{0:T(512)} %get-tuple-element.163) | copy-start | bytes 6148
  (6 other events, 4.8 us)
Sparse Core Ops, SparseCore 0:
  10.1 83.8 all-gather.3
  96.8 82.1 all-gather.5
  181.7 76.2 all-gather.7
  268.2 49.3 reduce-scatter.1
where the time goes:
time: 327 us; the launch traced here: 326 us
  waiting for transfers between devices  122 us (37%)
  blocking collectives  76.9 us (24%)
  starting transfers between devices  40.3 us (12%)
  matrix products  35.9 us (11%)
  other arithmetic  21.5 us (7%)
  local copies, waits for them, and re-layouts  14.6 us (4%)
  between operations  13.3 us (4%)
    ppermute x9, waiting for transfers between devices, passed_along(): return lax.ppermute(array, axis, pairs)  69.4 us
    psum x1, blocking collectives, shards(): hidden_full = lax.psum(projected + placed, 'head').astype(jnp.bfloat16)  67.1 us
    reduce_scatter x1, waiting for transfers between devices, shards(): lax.psum_scatter(down_out.astype(jnp.bfloat16), 'head', scatter_dimension...  49.5 us
    ppermute x9, starting transfers between devices, passed_along(): return lax.ppermute(array, axis, pairs)  40.1 us
    dot_general x1, matrix products, shards(): jnp.dot(columns, lax.all_gather(down_weight, 'ctx', axis=0, tiled=True),...  9.99 us
    psum x1, blocking collectives, shards(): squares = lax.psum(jnp.sum(gated * gated, axis=1), 'head')  9.76 us
    dot_general x1, matrix products, shards(): jnp.dot(columns, lax.all_gather(out_weight, 'ctx', axis=0, tiled=True), p...  7.13 us
  transfers between devices with their start and end apart: 13, of which 11 were waited for; matrix products, arithmetic and copies ran while one was open for 18% of the time, Pallas kernels for 0%

commit v1 on v0

--- a/solution.py
+++ b/solution.py
@@ -1,3 +1,4 @@
+import functools
 import jax
 import jax.numpy as jnp
 from jax import lax
@@ -9,6 +10,14 @@
 DOC_GROUPS = 16
 INNER = 4096
 EPS = 1e-05
+
+
+def close_orders(frame, peer_axis):
+    f_now = lax.all_gather(frame, axis_name=peer_axis)
+    return jnp.sum(f_now, axis=0)
+
+
+switch_units_up = functools.partial(close_orders, peer_axis="head")
 
 
 def passed_along(array, axis, by):
@@ -122,7 +131,7 @@
     placed = lax.dynamic_update_slice_in_dim(
         jnp.zeros((tok_rows, width), jnp.float32), residual.astype(jnp.float32), offset, 1
     )
-    hidden_full = lax.psum(projected + placed, "head").astype(jnp.bfloat16)
+    hidden_full = switch_units_up(projected + placed).astype(jnp.bfloat16)
     hidden_wide = hidden_full.astype(jnp.float32)
     row_scale = lax.rsqrt(jnp.mean(hidden_wide * hidden_wide, axis=1) + EPS)
     scaled = (hidden_wide * row_scale[:, None] * mlp_gain).astype(jnp.bfloat16)

time: 327 us -> 557 us (1.70)
  waiting for transfers between devices: 122 us -> 414 us
  blocking collectives: 76.9 us -> 8.54 us
  other arithmetic: 21.5 us -> 27.4 us
    all_gather x0 -> x1, waiting for transfers between devices: none -> 171 us  [close_orders(): f_now = lax.all_gather(frame, axis_name=peer_axis)]
    all_gather x1, waiting for transfers between devices: 0.02 us -> 78.7 us  [sent_together(): filled = lax.all_gather(both, axis, axis=dim, tiled=True)]
    all_gather x1, waiting for transfers between devices: 1.32 us -> 72.6 us  [shards(): lax.all_gather(down_weight, 'ctx', axis=0, tiled=True)]
    psum x1 -> x0, blocking collectives: 67.1 us -> none  [shards(): hidden_full = lax.psum(projected + placed, 'head').astype(jnp.bfloat16)]
    reduce_scatter x1, waiting for transfers between devices: 49.5 us -> 29.2 us  [shards(): lax.psum_scatter(down_out.astype(jnp.bfloat16), 'head', scatter_dimension...]
    reduce_sum x0 -> x1, other arithmetic: none -> 8.11 us  [close_orders(): return jnp.sum(f_now, axis=0)]
    ppermute x9, waiting for transfers between devices: 69.4 us -> 61.4 us  [passed_along(): return lax.ppermute(array, axis, pairs)]
  transfers between devices with their start and end apart: 13 -> 14, of which waited for: 11 -> 13; matrix products, arithmetic and copies ran while one was open for 18% -> 10% of each run, Pallas kernels for 0% -> 0%
where the time goes in v1:
time: 557 us; the launch traced here: 556 us
  waiting for transfers between devices  414 us (74%)
  starting transfers between devices  40.5 us (7%)
  matrix products  33.7 us (6%)
  other arithmetic  27.4 us (5%)
  local copies, waits for them, and re-layouts  17.1 us (3%)
  between operations  13.3 us (2%)
  blocking collectives  8.54 us (2%)
    all_gather x1, waiting for transfers between devices, close_orders(): f_now = lax.all_gather(frame, axis_name=peer_axis)  171 us
    all_gather x1, waiting for transfers between devices, sent_together(): filled = lax.all_gather(both, axis, axis=dim, tiled=True)  78.7 us
    all_gather x1, waiting for transfers between devices, shards(): lax.all_gather(down_weight, 'ctx', axis=0, tiled=True)  72.6 us
    ppermute x9, waiting for transfers between devices, passed_along(): return lax.ppermute(array, axis, pairs)  61.4 us
    ppermute x9, starting transfers between devices, passed_along(): return lax.ppermute(array, axis, pairs)  40.1 us
    reduce_scatter x1, waiting for transfers between devices, shards(): lax.psum_scatter(down_out.astype(jnp.bfloat16), 'head', scatter_dimension...  29.2 us
  transfers between devices with their start and end apart: 14, of which 13 were waited for; matrix products, arithmetic and copies ran while one was open for 10% of the time, Pallas kernels for 0%

profile of v1, /device:TPU:1, one launch (start us, length us, event | category | flops | bytes accessed | tf_op | source)
XLA Modules:
  0.0 556.1 jit_solution(13999388936519057593)
XLA Ops:
  12.7 27.5 %while.26 = (s32[]{:T(128)}, f32[2,256,16,64]{1,3,2,0:T(8,128)}, f32[2,16,128,64]{2,3,1,0:T(8,128)S(1)}, f32[2,16,256]{2,1,0:T(8,128)}, f32[2,16]{1,0:T(2,128)},...) while((s32[]{:T(128)}, f32[2,256,16,64]{1,3,2,0:T(8,128)}, ...), condition=%wide.region_5.6_spmd, body=%wide.region_0.5_spmd.sunk | while | flops 225981504 | bytes 7140167 | solution.py:93
  19.5 3.2 fusion.76
  33.3 3.1 fusion.76
  42.7 102.8 %while.27 = (s32[]{:T(128)}, f32[16,128,64]{1,2,0:T(8,128)S(1)}, f32[16]{0:T(128)S(1)}, f32[16,128,64]{1,2,0:T(8,128)S(1)}, s32[]{:T(128)}) while((s32[]{:T(128)}, f32[16,128,64]{1,2,0:T(8,128)S(1)}, f32[16]{0:T(128)S(1)}, f32[16,128,64]{1,2,0:T(8,128)S(1)}, s32[]{:T(128)}) %tuple.50), condition=%wide.region_7.8_spmd, body=%wide.region_6.7_spmd.sunk | while | flops 262146 | bytes 3670181 | solution.py:108
  42.8 4.9 collective-permute-start
  47.7 6.3 %collective-permute-done = f32[16,128,64]{1,2,0:T(8,128)S(1)} collective-permute-done((f32[16,128,64]{1,2,0:T(8,128)S(1)}, f32[16,128,64]{1,2,0:T(8,128)S(1)}, u32[]{:S(2)}, u32[]{:S(2)}) %collective-permute-start) | collective-permute-done | bytes 524320 | tf_op jit(solution)/shard_map/while/body/eval_jaxpr/ppermute | solution.py:26
  54.1 4.4 collective-permute-start
  58.5 7.5 %collective-permute-done = f32[16,128,64]{1,2,0:T(8,128)S(1)} collective-permute-done((f32[16,128,64]{1,2,0:T(8,128)S(1)}, f32[16,128,64]{1,2,0:T(8,128)S(1)}, u32[]{:S(2)}, u32[]{:S(2)}) %collective-permute-start) | collective-permute-done | bytes 524320 | tf_op jit(solution)/shard_map/while/body/eval_jaxpr/ppermute | solution.py:26
  66.1 4.4 collective-permute-start
  70.5 9.6 %collective-permute-done = f32[16,128,64]{1,2,0:T(8,128)S(1)} collective-permute-done((f32[16,128,64]{1,2,0:T(8,128)S(1)}, f32[16,128,64]{1,2,0:T(8,128)S(1)}, u32[]{:S(2)}, u32[]{:S(2)}) %collective-permute-start) | collective-permute-done | bytes 524320 | tf_op jit(solution)/shard_map/while/body/eval_jaxpr/ppermute | solution.py:26
  80.3 4.5 collective-permute-start
  84.8 7.5 %collective-permute-done = f32[16,128,64]{1,2,0:T(8,128)S(1)} collective-permute-done((f32[16,128,64]{1,2,0:T(8,128)S(1)}, f32[16,128,64]{1,2,0:T(8,128)S(1)}, u32[]{:S(2)}, u32[]{:S(2)}) %collective-permute-start) | collective-permute-done | bytes 524320 | tf_op jit(solution)/shard_map/while/body/eval_jaxpr/ppermute | solution.py:26
  92.4 4.4 collective-permute-start
  96.8 6.1 %collective-permute-done = f32[16,128,64]{1,2,0:T(8,128)S(1)} collective-permute-done((f32[16,128,64]{1,2,0:T(8,128)S(1)}, f32[16,128,64]{1,2,0:T(8,128)S(1)}, u32[]{:S(2)}, u32[]{:S(2)}) %collective-permute-start) | collective-permute-done | bytes 524320 | tf_op jit(solution)/shard_map/while/body/eval_jaxpr/ppermute | solution.py:26
  103.1 4.4 collective-permute-start
  107.5 6.1 %collective-permute-done = f32[16,128,64]{1,2,0:T(8,128)S(1)} collective-permute-done((f32[16,128,64]{1,2,0:T(8,128)S(1)}, f32[16,128,64]{1,2,0:T(8,128)S(1)}, u32[]{:S(2)}, u32[]{:S(2)}) %collective-permute-start) | collective-permute-done | bytes 524320 | tf_op jit(solution)/shard_map/while/body/eval_jaxpr/ppermute | solution.py:26
  113.7 4.4 collective-permute-start
  118.1 6.1 %collective-permute-done = f32[16,128,64]{1,2,0:T(8,128)S(1)} collective-permute-done((f32[16,128,64]{1,2,0:T(8,128)S(1)}, f32[16,128,64]{1,2,0:T(8,128)S(1)}, u32[]{:S(2)}, u32[]{:S(2)}) %collective-permute-start) | collective-permute-done | bytes 524320 | tf_op jit(solution)/shard_map/while/body/eval_jaxpr/ppermute | solution.py:26
  124.3 4.4 collective-permute-start
  128.7 6.1 %collective-permute-done = f32[16,128,64]{1,2,0:T(8,128)S(1)} collective-permute-done((f32[16,128,64]{1,2,0:T(8,128)S(1)}, f32[16,128,64]{1,2,0:T(8,128)S(1)}, u32[]{:S(2)}, u32[]{:S(2)}) %collective-permute-start) | collective-permute-done | bytes 524320 | tf_op jit(solution)/shard_map/while/body/eval_jaxpr/ppermute | solution.py:26
  134.9 4.4 collective-permute-start
  139.3 6.1 %collective-permute-done = f32[16,128,64]{1,2,0:T(8,128)S(1)} collective-permute-done((f32[16,128,64]{1,2,0:T(8,128)S(1)}, f32[16,128,64]{1,2,0:T(8,128)S(1)}, u32[]{:S(2)}, u32[]{:S(2)}) %collective-permute-start) | collective-permute-done | bytes 524320 | tf_op jit(solution)/shard_map/while/body/eval_jaxpr/ppermute | solution.py:26
  150.2 2.0 copy.49
  152.9 8.5 %psum.7 = f32[512]{0:T(512)S(1)} all-reduce(f32[512]{0:T(512)S(1)} %multiply_reduce_fusion.1), channel_id=1, replica_groups=mesh['ctx'=64,'head'=4] {'head'}, use_global_device_ids=true, to_apply=%region_9.10 | all-reduce | flops 512 | bytes 4096 | tf_op jit(solution)/shard_map/psum | solution.py:120
  161.5 5.0 fusion.40
  172.1 170.6 %all-gather.7.cloned.1.call-done = f32[4,512,2048]{2,1,0:T(8,128)} async-done(((f32[1,512,2048]{2,1,0:T(8,128)}), f32[4,512,2048]{2,1,0:T(8,128)}) %all-gather.7.cloned.1.call-update) | async-done | bytes 16777232 | tf_op jit(solution)/shard_map/all_gather | solution.py:16
  342.6 8.1 %reduce_sum.28 = bf16[512,2048]{1,0:T(8,128)(2,1)S(1)} reduce(f32[4,512,2048]{2,1,0:T(8,128)} %all-gather.7.cloned.1.call-done, f32[]{:T(128)} %constant.33.clone.1), dimensions={0}, to_apply=%region_10.11 | reduce | flops 3145728 | bytes 18874372 | tf_op jit(solution)/shard_map/reduce_sum | solution.py:17
  351.3 78.7 %all-gather.9.cloned.1.call-done = bf16[2048,2048]{1,0:T(8,128)(2,1)} async-done(((bf16[32,2048]{1,0:T(8,128)(2,1)}), bf16[2048,2048]{1,0:T(8,128)(2,1)}) %all-gather.9.cloned.1.call-update) | async-done | bytes 8388624 | tf_op jit(solution)/shard_map/all_gather | solution.py:32
  430.0 5.9 %fusion.26 = f32[512,1024]{1,0:T(8,128)} fusion(bf16[2048,2048]{1,0:T(8,128)(2,1)} %all-gather.9.cloned.1.call-done, bf16[512,2048]{1,0:T(8,128)(2,1)S(1)} %reduce_sum.28, f32[2048]{0:T(1024)S(1)} %copy-done.16, f32[512]{0:T(512)S(1)} %add_rsqrt_fusion), kind=kOutput, calls=%fused_computation.49 | convolution fusion | flops 2151677952 | bytes 8398848 | tf_op jit(solution)/shard_map/dot_general | solution.py:141
  435.8 72.6 %all-gather.11.cloned.1.call-done = bf16[1024,2048]{1,0:T(8,128)(2,1)} async-done(((bf16[16,2048]{1,0:T(8,128)(2,1)}), bf16[1024,2048]{1,0:T(8,128)(2,1)}) %all-gather.11.cloned.1.call-update) | async-done | bytes 4194320 | tf_op jit(solution)/shard_map/all_gather | solution.py:147
  508.4 10.0 %convolution_convert_fusion = bf16[512,2048]{1,0:T(8,128)(2,1)} fusion(bf16[1024,2048]{1,0:T(8,128)(2,1)} %all-gather.11.cloned.1.call-done, f32[512,1024]{1,0:T(8,128)} %fusion.26, bf16[2048,2048]{1,0:T(8,128)(2,1)} %all-gather.9.cloned.1.call-done, bf16[512,2048]{1,0:T(8,128)(2,1)S(1)} %reduce_sum.28, f32[2048]{0:T(1024)S(1)} %copy-done.16, ...), kind=kOutput, calls=%fused_computation.51 | convolution fusion | flops 4303355904 | bytes 14690304 | tf_op jit(solution)/shard_map/dot_general | solution.py:145
  518.4 29.2 %reduce-scatter.2.cloned.1.call-done = bf16[512,512]{1,0:T(8,128)(2,1)} async-done(((bf16[512,2048]{1,0:T(8,128)(2,1)}), bf16[512,512]{1,0:T(8,128)(2,1)}) %reduce-scatter.2.cloned.1.call-update) | async-done | bytes 524304 | tf_op jit(solution)/shard_map/reduce_scatter | solution.py:150
  (154 shorter events, 42.5 us)
Async XLA Ops:
  6.5 6.1 %copy-start = (bf16[512,128]{1,0:T(8,128)(2,1)S(1)}, bf16[512,128]{1,0:T(8,128)(2,1)}, u32[]{:S(2)}) copy-start(bf16[512,128]{1,0:T(8,128)(2,1)} %param.21) | copy-start | bytes 393220
  6.5 154.9 %all-gather.5.cloned.1.call-start = ((), (), s32[]{:S(2)}) async-start(), calls=%async_computation.1 | async-start | bytes 4259840 | tf_op jit(solution)/shard_map/all_gather | solution.py:126
  7.3 335.4 %all-gather.7.cloned.1.call-start = ((), (), s32[]{:S(2)}) async-start(), calls=%async_computation.2 | async-start | bytes 20971520 | tf_op jit(solution)/shard_map/all_gather | solution.py:16
  19.5 3.2 copy-start.7
  19.5 4.5 copy-start.4
  19.5 6.2 %copy-start.14 = (f32[2,16]{1,0:T(2,128)S(1)}, f32[2,16]{1,0:T(2,128)}, u32[]{:S(2)}) copy-start(f32[2,16]{1,0:T(2,128)} %get-tuple-element.291) | copy-start | bytes 388 | tf_op jit(solution)/shard_map/while
  19.5 6.3 %copy-start.2 = (f32[16,2,128]{2,0,1:T(8,128)S(1)}, f32[16,2,128]{2,0,1:T(8,128)}, u32[]{:S(2)}) copy-start(f32[16,2,128]{2,0,1:T(8,128)} %get-tuple-element.266) | copy-start | bytes 49156 | tf_op jit(solution)/shard_map/while
  19.5 6.3 %copy-start.8 = (f32[256]{0:T(256)S(1)}, f32[256]{0:T(256)}, u32[]{:S(2)}) copy-start(f32[256]{0:T(256)} %get-tuple-element.267) | copy-start | bytes 3076 | tf_op jit(solution)/shard_map/while
  19.5 6.3 %copy-start.11 = (f32[2,16,256]{2,1,0:T(8,128)S(1)}, f32[2,16,256]{2,1,0:T(8,128)}, u32[]{:S(2)}) copy-start(f32[2,16,256]{2,1,0:T(8,128)} %get-tuple-element.290) | copy-start | bytes 98308 | tf_op jit(solution)/shard_map/while
  33.2 3.2 copy-start.7
  33.2 4.4 copy-start.4
  33.2 6.2 %copy-start.14 = (f32[2,16]{1,0:T(2,128)S(1)}, f32[2,16]{1,0:T(2,128)}, u32[]{:S(2)}) copy-start(f32[2,16]{1,0:T(2,128)} %get-tuple-element.291) | copy-start | bytes 388 | tf_op jit(solution)/shard_map/while
  33.3 6.2 %copy-start.2 = (f32[16,2,128]{2,0,1:T(8,128)S(1)}, f32[16,2,128]{2,0,1:T(8,128)}, u32[]{:S(2)}) copy-start(f32[16,2,128]{2,0,1:T(8,128)} %get-tuple-element.266) | copy-start | bytes 49156 | tf_op jit(solution)/shard_map/while
  33.3 6.3 %copy-start.8 = (f32[256]{0:T(256)S(1)}, f32[256]{0:T(256)}, u32[]{:S(2)}) copy-start(f32[256]{0:T(256)} %get-tuple-element.267) | copy-start | bytes 3076 | tf_op jit(solution)/shard_map/while
  33.3 6.3 %copy-start.11 = (f32[2,16,256]{2,1,0:T(8,128)S(1)}, f32[2,16,256]{2,1,0:T(8,128)}, u32[]{:S(2)}) copy-start(f32[2,16,256]{2,1,0:T(8,128)} %get-tuple-element.290) | copy-start | bytes 98308 | tf_op jit(solution)/shard_map/while
  42.8 11.2 %collective-permute-start = (f32[16,128,64]{1,2,0:T(8,128)S(1)}, f32[16,128,64]{1,2,0:T(8,128)S(1)}, u32[]{:S(2)}, u32[]{:S(2)}) collective-permute-start(f32[16,128,64]{1,2,0:T(8,128)S(1)} %multiply_add_fusion.2), channel_id=1, source_target_pairs={{0,4},{4,8},{8,12},{12,16},{16,20},{20,24},{24,28},{28,32},{32,36}... | collective-permute-start | bytes 1572872 | tf_op jit(solution)/shard_map/while/body/eval_jaxpr/ppermute | solution.py:26
  54.1 11.9 %collective-permute-start = (f32[16,128,64]{1,2,0:T(8,128)S(1)}, f32[16,128,64]{1,2,0:T(8,128)S(1)}, u32[]{:S(2)}, u32[]{:S(2)}) collective-permute-start(f32[16,128,64]{1,2,0:T(8,128)S(1)} %multiply_add_fusion.2), channel_id=1, source_target_pairs={{0,4},{4,8},{8,12},{12,16},{16,20},{20,24},{24,28},{28,32},{32,36}... | collective-permute-start | bytes 1572872 | tf_op jit(solution)/shard_map/while/body/eval_jaxpr/ppermute | solution.py:26
  66.1 14.0 %collective-permute-start = (f32[16,128,64]{1,2,0:T(8,128)S(1)}, f32[16,128,64]{1,2,0:T(8,128)S(1)}, u32[]{:S(2)}, u32[]{:S(2)}) collective-permute-start(f32[16,128,64]{1,2,0:T(8,128)S(1)} %multiply_add_fusion.2), channel_id=1, source_target_pairs={{0,4},{4,8},{8,12},{12,16},{16,20},{20,24},{24,28},{28,32},{32,36}... | collective-permute-start | bytes 1572872 | tf_op jit(solution)/shard_map/while/body/eval_jaxpr/ppermute | solution.py:26
  80.3 12.0 %collective-permute-start = (f32[16,128,64]{1,2,0:T(8,128)S(1)}, f32[16,128,64]{1,2,0:T(8,128)S(1)}, u32[]{:S(2)}, u32[]{:S(2)}) collective-permute-start(f32[16,128,64]{1,2,0:T(8,128)S(1)} %multiply_add_fusion.2), channel_id=1, source_target_pairs={{0,4},{4,8},{8,12},{12,16},{16,20},{20,24},{24,28},{28,32},{32,36}... | collective-permute-start | bytes 1572872 | tf_op jit(solution)/shard_map/while/body/eval_jaxpr/ppermute | solution.py:26
  92.4 10.5 %collective-permute-start = (f32[16,128,64]{1,2,0:T(8,128)S(1)}, f32[16,128,64]{1,2,0:T(8,128)S(1)}, u32[]{:S(2)}, u32[]{:S(2)}) collective-permute-start(f32[16,128,64]{1,2,0:T(8,128)S(1)} %multiply_add_fusion.2), channel_id=1, source_target_pairs={{0,4},{4,8},{8,12},{12,16},{16,20},{20,24},{24,28},{28,32},{32,36}... | collective-permute-start | bytes 1572872 | tf_op jit(solution)/shard_map/while/body/eval_jaxpr/ppermute | solution.py:26
  103.1 10.5 %collective-permute-start = (f32[16,128,64]{1,2,0:T(8,128)S(1)}, f32[16,128,64]{1,2,0:T(8,128)S(1)}, u32[]{:S(2)}, u32[]{:S(2)}) collective-permute-start(f32[16,128,64]{1,2,0:T(8,128)S(1)} %multiply_add_fusion.2), channel_id=1, source_target_pairs={{0,4},{4,8},{8,12},{12,16},{16,20},{20,24},{24,28},{28,32},{32,36}... | collective-permute-start | bytes 1572872 | tf_op jit(solution)/shard_map/while/body/eval_jaxpr/ppermute | solution.py:26
  113.7 10.5 %collective-permute-start = (f32[16,128,64]{1,2,0:T(8,128)S(1)}, f32[16,128,64]{1,2,0:T(8,128)S(1)}, u32[]{:S(2)}, u32[]{:S(2)}) collective-permute-start(f32[16,128,64]{1,2,0:T(8,128)S(1)} %multiply_add_fusion.2), channel_id=1, source_target_pairs={{0,4},{4,8},{8,12},{12,16},{16,20},{20,24},{24,28},{28,32},{32,36}... | collective-permute-start | bytes 1572872 | tf_op jit(solution)/shard_map/while/body/eval_jaxpr/ppermute | solution.py:26
  124.3 10.5 %collective-permute-start = (f32[16,128,64]{1,2,0:T(8,128)S(1)}, f32[16,128,64]{1,2,0:T(8,128)S(1)}, u32[]{:S(2)}, u32[]{:S(2)}) collective-permute-start(f32[16,128,64]{1,2,0:T(8,128)S(1)} %multiply_add_fusion.2), channel_id=1, source_target_pairs={{0,4},{4,8},{8,12},{12,16},{16,20},{20,24},{24,28},{28,32},{32,36}... | collective-permute-start | bytes 1572872 | tf_op jit(solution)/shard_map/while/body/eval_jaxpr/ppermute | solution.py:26
  134.9 10.5 %collective-permute-start = (f32[16,128,64]{1,2,0:T(8,128)S(1)}, f32[16,128,64]{1,2,0:T(8,128)S(1)}, u32[]{:S(2)}, u32[]{:S(2)}) collective-permute-start(f32[16,128,64]{1,2,0:T(8,128)S(1)} %multiply_add_fusion.2), channel_id=1, source_target_pairs={{0,4},{4,8},{8,12},{12,16},{16,20},{20,24},{24,28},{28,32},{32,36}... | collective-permute-start | bytes 1572872 | tf_op jit(solution)/shard_map/while/body/eval_jaxpr/ppermute | solution.py:26
  150.2 2.0 copy-start.3
  152.2 9.3 %copy-start.17 = (f32[1024]{0:T(1024)S(1)}, f32[1024]{0:T(1024)}, u32[]{:S(2)}) copy-start(f32[1024]{0:T(1024)} %param.27) | copy-start | bytes 12292
  166.5 2.0 copy-start.5
  169.7 260.2 %all-gather.9.cloned.1.call-start = ((), (), s32[]{:S(2)}) async-start(), calls=%async_computation.3 | async-start | bytes 8519680 | tf_op jit(solution)/shard_map/all_gather | solution.py:32
  171.3 337.2 %all-gather.11.cloned.1.call-start = ((), (), s32[]{:S(2)}) async-start(), calls=%async_computation.4 | async-start | bytes 4259840 | tf_op jit(solution)/shard_map/all_gather | solution.py:147
  171.8 375.8 %reduce-scatter.2.cloned.1.call-start = ((), (), s32[]{:S(2)}) async-start(), calls=%async_computation.5 | async-start | bytes 2621440 | tf_op jit(solution)/shard_map/reduce_scatter | solution.py:150
  350.8 79.2 %copy-start.16 = (f32[2048]{0:T(1024)S(1)}, f32[2048]{0:T(1024)}, u32[]{:S(2)}) copy-start(f32[2048]{0:T(1024)} %param.30) | copy-start | bytes 24580
  518.4 29.2 %copy-start.13 = (f32[512]{0:T(512)S(1)}, f32[512]{0:T(512)}, u32[]{:S(2)}) copy-start(f32[512]{0:T(512)} %get-tuple-element.163) | copy-start | bytes 6148
  (9 other events, 9.6 us)
Sparse Core Ops, SparseCore 0:
  10.1 83.6 all-gather.4
  169.9 172.7 all-gather.6
  345.4 84.4 all-gather.8
  432.6 75.7 all-gather.10
  518.5 29.0 reduce-scatter.1
